TPU v7x, 32 devices: a whole 2x2x4 slice. The times are simulated.
32 devices in a mesh: dp: 2 (over core), ctx: 4 (over z), fsdp: 4 (over y, x).
Axes of the slice: x: 2, y: 2, z: 4, core: 2. Of those that a mesh axis runs over, the one named last changes fastest.
Arguments:
- tokens: bfloat16 [8, 2, 1024, 2048], P(('dp', 'fsdp'), None, 'ctx'), may hold values from -6 to 6
- cotangent: bfloat16 [8, 2, 1024, 2048], P(('dp', 'fsdp'), None, 'ctx'), may hold values from -6 to 6
- lengths: int32 [8, 2], P(('dp', 'fsdp')), may hold values from 513 to 1024, as said below
- deal: int32 [8, 2, 8], P(('dp', 'fsdp')), may hold values from 0 to 7, each once within a row
- ln_gain: bfloat16 [2048], P('fsdp'), may hold values from 0.5 to 1.5
- ln_bias: bfloat16 [2048], P('fsdp'), may hold values from -1 to 1
- w_qkv: bfloat16 [2048, 6144], P('fsdp'), may hold values from -0.125 to 0.125
- b_qkv: bfloat16 [6144], P('fsdp'), may hold values from -1 to 1
- w_out: bfloat16 [2048, 2048], P('fsdp'), may hold values from -3 to 3
- b_out: bfloat16 [2048], P('fsdp'), may hold values from -2.5 to 2.5
- w_up: bfloat16 [2048, 8192], P('fsdp'), may hold values from -0.125 to 0.125
- b_up: bfloat16 [8192], P('fsdp'), may hold values from -1 to 1
- w_down: bfloat16 [8192, 2048], P('fsdp'), may hold values from -0.0625 to 0.0625
- b_down: bfloat16 [2048], P('fsdp'), may hold values from -2.5 to 2.5
Outputs:
- outputs: bfloat16 [8, 2, 1024, 2048], P(('dp', 'fsdp'), None, 'ctx')
- input_grad: bfloat16 [8, 2, 1024, 2048], P(('dp', 'fsdp'), None, 'ctx')
- grad_ln_gain: float32 [2048], P('fsdp')
- grad_ln_bias: float32 [2048], P('fsdp')
- grad_w_qkv: float32 [2048, 6144], P('fsdp')
- grad_b_qkv: float32 [6144], P('fsdp')
- grad_w_out: float32 [2048, 2048], P('fsdp')
- grad_b_out: float32 [2048], P('fsdp')
- grad_w_up: float32 [2048, 8192], P('fsdp')
- grad_b_up: float32 [8192], P('fsdp')
- grad_w_down: float32 [8192, 2048], P('fsdp')
- grad_b_down: float32 [2048], P('fsdp')
Inputs may be any that keep to these rules, and one draw needn't show every extreme that they name: lengths[g, m] tokens fill the first positions of a sequence, the rest is padding; in every draw one sequence is exactly 1024 long and one exactly 513. Each row of deal is a permutation of the 8 blocks of a sequence.
All inputs are finite; a program needn't handle non-finite values.
Results may differ from a plain program's by a relative error of at most 0.02.
Values may be sent and summed in bfloat16 or wider, within the bound.
No kernel may reach another device: no remote copies, remote signals or barrier semaphores. Data moves between devices by JAX's collectives and lax.ppermute only.
A program may use at most 832 MiB of HBM per device.

v0:
```python
import jax
import jax.numpy as jnp
from jax import lax
from jax.sharding import PartitionSpec as P

HEAD_DIM = 64
ROT = 32
EPS = 1e-05
BASE = 10000.0


def contract_rows(left, right):
    return lax.dot_general(
        left, right, (((0,), (0,)), ((), ())), preferred_element_type=jnp.float32
    )


def contract_cols(left, right):
    return lax.dot_general(
        left, right, (((1,), (1,)), ((), ())), preferred_element_type=jnp.float32
    )


def angles_of(positions):
    half = ROT // 2
    freqs = BASE ** (-(jnp.arange(half, dtype=jnp.float32) * 2.0) / ROT)
    angles = positions.astype(jnp.float32)[:, None] * freqs[None, :]
    return (jnp.cos(angles)[:, None, :], jnp.sin(angles)[:, None, :])


def rotate(values, cosine, sine):
    half = ROT // 2
    first = values[..., :half]
    second = values[..., half:ROT]
    return jnp.concatenate(
        [first * cosine - second * sine, second * cosine + first * sine, values[..., ROT:]], axis=-1
    )


def rotate_back(values, cosine, sine):
    half = ROT // 2
    first = values[..., :half]
    second = values[..., half:ROT]
    return jnp.concatenate(
        [first * cosine + second * sine, second * cosine - first * sine, values[..., ROT:]], axis=-1
    )


def layer_step(weights, inputs, upstream, length, deal_row):
    gain, shift, w_qkv, b_qkv, w_out, b_out, w_up, b_up, w_down, b_down = weights
    row_count, width = inputs.shape
    block_rows = row_count // 2
    head_count = width // HEAD_DIM
    scale = HEAD_DIM ** (-0.5)
    place = lax.axis_index("ctx")
    offsets = jnp.arange(block_rows, dtype=jnp.int32)
    own_blocks = lax.dynamic_slice_in_dim(deal_row, 2 * place, 2)
    local_pos = (own_blocks[:, None] * block_rows + offsets[None, :]).reshape(row_count)
    every_pos = (deal_row[:, None] * block_rows + offsets[None, :]).reshape(-1)
    valid = (local_pos < length).astype(jnp.float32)[:, None]
    allowed = (every_pos[None, :] <= local_pos[:, None]) & (every_pos[None, :] < length)
    cosine, sine = angles_of(local_pos)
    inputs_f = inputs.astype(jnp.float32)
    gain_f = gain.astype(jnp.float32)
    centered = inputs_f - jnp.mean(inputs_f, axis=-1, keepdims=True)
    variance = jnp.mean(centered * centered, axis=-1, keepdims=True)
    inv_std = lax.rsqrt(variance + EPS)
    normed = centered * inv_std
    hidden = (normed * gain_f + shift.astype(jnp.float32)).astype(jnp.bfloat16)
    joined = jnp.dot(hidden, w_qkv, preferred_element_type=jnp.float32) + b_qkv.astype(jnp.float32)
    query = (
        rotate(joined[:, :width].reshape(row_count, head_count, HEAD_DIM), cosine, sine)
        .reshape(row_count, width)
        .astype(jnp.bfloat16)
    )
    keyed = (
        rotate(joined[:, width : 2 * width].reshape(row_count, head_count, HEAD_DIM), cosine, sine)
        .reshape(row_count, width)
        .astype(jnp.bfloat16)
    )
    valued = joined[:, 2 * width :].astype(jnp.bfloat16)
    keys_all, values_all = (
        lax.all_gather(keyed, "ctx", axis=0, tiled=True),
        lax.all_gather(valued, "ctx", axis=0, tiled=True),
    )
    total_keys = keys_all.shape[0]
    group = min(8, head_count)
    span = group * HEAD_DIM

    def heads_of(array, start, count):
        return array[:, start : start + span].reshape(count, group, HEAD_DIM)

    def block_scores(start):
        raw = (
            jnp.einsum(
                "qhd,khd->hqk",
                heads_of(query, start, row_count),
                heads_of(keys_all, start, total_keys),
                preferred_element_type=jnp.float32,
            )
            * scale
        )
        return jnp.where(allowed[None], raw, -1e30)

    attended_parts = []
    lse_parts = []
    for start in range(0, width, span):
        masked = block_scores(start)
        highest = jnp.max(masked, axis=-1, keepdims=True)
        expo = jnp.exp(masked - highest)
        total = jnp.sum(expo, axis=-1, keepdims=True)
        weights_low = (expo / total).astype(jnp.bfloat16)
        mixed = jnp.einsum(
            "hqk,khd->qhd",
            weights_low,
            heads_of(values_all, start, total_keys),
            preferred_element_type=jnp.float32,
        )
        attended_parts.append(mixed.reshape(row_count, span))
        lse_parts.append(highest + jnp.log(total))
    attended = jnp.concatenate(attended_parts, axis=1).astype(jnp.bfloat16)
    branch = jnp.dot(attended, w_out, preferred_element_type=jnp.float32) + b_out.astype(
        jnp.float32
    )
    upward = jnp.dot(hidden, w_up, preferred_element_type=jnp.float32) + b_up.astype(jnp.float32)
    activated = jax.nn.gelu(upward, approximate=True).astype(jnp.bfloat16)
    feed = jnp.dot(activated, w_down, preferred_element_type=jnp.float32) + b_down.astype(
        jnp.float32
    )
    result = (valid * (inputs_f + branch + feed)).astype(jnp.bfloat16)
    grad_out = upstream.astype(jnp.float32) * valid
    grad_low = grad_out.astype(jnp.bfloat16)
    row_total = jnp.sum(grad_out, axis=0)
    d_down = contract_rows(activated, grad_low)
    d_wout = contract_rows(attended, grad_low)
    d_act = contract_cols(grad_low, w_down)
    _, gelu_pull = jax.vjp(lambda value: jax.nn.gelu(value, approximate=True), upward)
    d_upward = gelu_pull(d_act)[0].astype(jnp.bfloat16)
    d_wup = contract_rows(hidden, d_upward)
    d_bup = jnp.sum(d_upward.astype(jnp.float32), axis=0)
    d_attended = contract_cols(grad_low, w_out).astype(jnp.bfloat16)
    dq_parts = []
    dk_parts = []
    dv_parts = []
    delta_parts = []
    for index, start in enumerate(range(0, width, span)):
        masked = block_scores(start)
        probs = jnp.where(allowed[None], jnp.exp(masked - lse_parts[index]), 0.0)
        d_heads = heads_of(d_attended, start, row_count)
        d_probs = jnp.einsum(
            "qhd,khd->hqk",
            d_heads,
            heads_of(values_all, start, total_keys),
            preferred_element_type=jnp.float32,
        )
        delta = jnp.sum(probs * d_probs, axis=-1, keepdims=True)
        d_scores = (probs * (d_probs - delta)).astype(jnp.bfloat16)
        d_query = (
            jnp.einsum(
                "hqk,khd->qhd",
                d_scores,
                heads_of(keys_all, start, total_keys),
                preferred_element_type=jnp.float32,
            )
            * scale
        )
        dq_parts.append(d_query.reshape(row_count, span))
        delta_parts.append(delta[:, :, 0].T)
        d_keyed = (
            jnp.einsum(
                "hqk,qhd->khd",
                d_scores,
                heads_of(query, start, row_count),
                preferred_element_type=jnp.float32,
            )
            * scale
        )
        d_valued = jnp.einsum(
            "hqk,qhd->khd", probs.astype(jnp.bfloat16), d_heads, preferred_element_type=jnp.float32
        )
        dk_parts.append(d_keyed.reshape(total_keys, span))
        dv_parts.append(d_valued.reshape(total_keys, span))
    keys_grad_all = jnp.concatenate(dk_parts, axis=1)
    values_grad_all = jnp.concatenate(dv_parts, axis=1)
    keys_grad, values_grad = (
        lax.psum_scatter(
            keys_grad_all.astype(jnp.bfloat16), "ctx", scatter_dimension=0, tiled=True
        ).astype(jnp.float32),
        lax.psum_scatter(
            values_grad_all.astype(jnp.bfloat16), "ctx", scatter_dimension=0, tiled=True
        ).astype(jnp.float32),
    )
    query_grad = rotate_back(
        jnp.concatenate(dq_parts, axis=1).reshape(row_count, head_count, HEAD_DIM), cosine, sine
    ).reshape(row_count, width)
    keyed_grad = rotate_back(
        keys_grad.reshape(row_count, head_count, HEAD_DIM), cosine, sine
    ).reshape(row_count, width)
    d_joined = jnp.concatenate([query_grad, keyed_grad, values_grad], axis=1).astype(jnp.bfloat16)
    d_wqkv = contract_rows(hidden, d_joined)
    d_bqkv = jnp.sum(d_joined.astype(jnp.float32), axis=0)
    d_hidden = contract_cols(d_joined, w_qkv) + contract_cols(d_upward, w_up)
    d_gain = jnp.sum(d_hidden * normed, axis=0)
    d_shift = jnp.sum(d_hidden, axis=0)
    d_norm = d_hidden * gain_f
    d_inputs = inv_std * (
        d_norm
        - jnp.mean(d_norm, axis=-1, keepdims=True)
        - normed * jnp.mean(d_norm * normed, axis=-1, keepdims=True)
    )
    back = (grad_out + d_inputs).astype(jnp.bfloat16)
    return (
        result,
        back,
        (d_gain, d_shift, d_wqkv, d_bqkv, d_wout, row_total, d_wup, d_bup, d_down, row_total),
    )


def body(
    tokens,
    cotangent,
    lengths,
    deal,
    ln_gain,
    ln_bias,
    w_qkv,
    b_qkv,
    w_out,
    b_out,
    w_up,
    b_up,
    w_down,
    b_down,
):
    shards = (ln_gain, ln_bias, w_qkv, b_qkv, w_out, b_out, w_up, b_up, w_down, b_down)
    shard_count = lax.axis_size("fsdp")
    summed = tuple(
        (
            jnp.zeros((piece.shape[0] * shard_count,) + piece.shape[1:], jnp.float32)
            for piece in shards
        )
    )
    results = []
    backs = []
    for micro_index in range(tokens.shape[1]):
        gathered = (
            lax.all_gather(ln_gain, "fsdp", axis=0, tiled=True),
            lax.all_gather(ln_bias, "fsdp", axis=0, tiled=True),
            lax.all_gather(w_qkv, "fsdp", axis=0, tiled=True),
            lax.all_gather(b_qkv, "fsdp", axis=0, tiled=True),
            lax.all_gather(w_out, "fsdp", axis=0, tiled=True),
            lax.all_gather(b_out, "fsdp", axis=0, tiled=True),
            lax.all_gather(w_up, "fsdp", axis=0, tiled=True),
            lax.all_gather(b_up, "fsdp", axis=0, tiled=True),
            lax.all_gather(w_down, "fsdp", axis=0, tiled=True),
            lax.all_gather(b_down, "fsdp", axis=0, tiled=True),
        )
        result, back, local = layer_step(
            gathered,
            tokens[0, micro_index],
            cotangent[0, micro_index],
            lengths[0, micro_index],
            deal[0, micro_index],
        )
        results.append(result)
        backs.append(back)
        summed = tuple((older + newer for older, newer in zip(summed, local)))
    summed = (
        lax.psum_scatter(
            summed[0].astype(jnp.bfloat16), "fsdp", scatter_dimension=0, tiled=True
        ).astype(jnp.float32),
        lax.psum_scatter(
            summed[1].astype(jnp.bfloat16), "fsdp", scatter_dimension=0, tiled=True
        ).astype(jnp.float32),
        lax.psum_scatter(
            summed[2].astype(jnp.bfloat16), "fsdp", scatter_dimension=0, tiled=True
        ).astype(jnp.float32),
        lax.psum_scatter(
            summed[3].astype(jnp.bfloat16), "fsdp", scatter_dimension=0, tiled=True
        ).astype(jnp.float32),
        lax.psum_scatter(
            summed[4].astype(jnp.bfloat16), "fsdp", scatter_dimension=0, tiled=True
        ).astype(jnp.float32),
        lax.psum_scatter(
            summed[5].astype(jnp.bfloat16), "fsdp", scatter_dimension=0, tiled=True
        ).astype(jnp.float32),
        lax.psum_scatter(
            summed[6].astype(jnp.bfloat16), "fsdp", scatter_dimension=0, tiled=True
        ).astype(jnp.float32),
        lax.psum_scatter(
            summed[7].astype(jnp.bfloat16), "fsdp", scatter_dimension=0, tiled=True
        ).astype(jnp.float32),
        lax.psum_scatter(
            summed[8].astype(jnp.bfloat16), "fsdp", scatter_dimension=0, tiled=True
        ).astype(jnp.float32),
        lax.psum_scatter(
            summed[9].astype(jnp.bfloat16), "fsdp", scatter_dimension=0, tiled=True
        ).astype(jnp.float32),
    )
    totals = (
        lax.psum(summed[0].astype(jnp.bfloat16), ("dp", "ctx")).astype(jnp.float32),
        lax.psum(summed[1].astype(jnp.bfloat16), ("dp", "ctx")).astype(jnp.float32),
        lax.psum(summed[2].astype(jnp.bfloat16), ("dp", "ctx")).astype(jnp.float32),
        lax.psum(summed[3].astype(jnp.bfloat16), ("dp", "ctx")).astype(jnp.float32),
        lax.psum(summed[4].astype(jnp.bfloat16), ("dp", "ctx")).astype(jnp.float32),
        lax.psum(summed[5].astype(jnp.bfloat16), ("dp", "ctx")).astype(jnp.float32),
        lax.psum(summed[6].astype(jnp.bfloat16), ("dp", "ctx")).astype(jnp.float32),
        lax.psum(summed[7].astype(jnp.bfloat16), ("dp", "ctx")).astype(jnp.float32),
        lax.psum(summed[8].astype(jnp.bfloat16), ("dp", "ctx")).astype(jnp.float32),
        lax.psum(summed[9].astype(jnp.bfloat16), ("dp", "ctx")).astype(jnp.float32),
    )
    stacked_out = jnp.stack(results)[None]
    stacked_back = jnp.stack(backs)[None]
    return (
        stacked_out,
        stacked_back,
        totals[0],
        totals[1],
        totals[2],
        totals[3],
        totals[4],
        totals[5],
        totals[6],
        totals[7],
        totals[8],
        totals[9],
    )


def solution(mesh):
    in_specs = (
        P(("dp", "fsdp"), None, "ctx", None),
        P(("dp", "fsdp"), None, "ctx", None),
        P(("dp", "fsdp"), None),
        P(("dp", "fsdp"), None, None),
        P("fsdp"),
        P("fsdp"),
        P("fsdp", None),
        P("fsdp"),
        P("fsdp", None),
        P("fsdp"),
        P("fsdp", None),
        P("fsdp"),
        P("fsdp", None),
        P("fsdp"),
    )
    out_specs = (
        P(("dp", "fsdp"), None, "ctx", None),
        P(("dp", "fsdp"), None, "ctx", None),
        P("fsdp"),
        P("fsdp"),
        P("fsdp", None),
        P("fsdp"),
        P("fsdp", None),
        P("fsdp"),
        P("fsdp", None),
        P("fsdp"),
        P("fsdp", None),
        P("fsdp"),
    )
    return jax.shard_map(body, mesh=mesh, in_specs=in_specs, out_specs=out_specs, check_vma=False)
```

profile of v0, /device:TPU:0, one launch (start us, length us, event | category | flops | bytes accessed | tf_op | source)
XLA Modules:
  0.0 3160.4 jit_solution(15819114740749781028)
XLA Ops:
  8.8 9.5 all-gather
  18.3 8.0 all-gather.1
  26.4 7.3 all-gather.2
  34.9 205.6 %all-gather.14.cloned.1.call-done = bf16[2048,6144]{1,0:T(8,128)(2,1)} async-done(((bf16[512,6144]{1,0:T(8,128)(2,1)}), bf16[2048,6144]{1,0:T(8,128)(2,1)}) %all-gather.14.cloned.1.call-update) | async-done | bytes 25165840 | tf_op jit(solution)/shard_map/all_gather | solution.py:249
  240.5 11.8 convolution_add_fusion.3
  256.3 11.8 convolution_add_fusion.2
  306.2 23.8 all-gather.20.cloned.1.call-done
  329.9 5.8 convolution_convert_fusion.1
  338.5 6.4 convolution_convert_fusion
  358.4 53.9 %all-gather.16.cloned.1.call-done = bf16[1024,2048]{1,0:T(8,128)(2,1)} async-done(((bf16[256,2048]{1,0:T(8,128)(2,1)}), bf16[1024,2048]{1,0:T(8,128)(2,1)}) %all-gather.16.cloned.1.call-update) | async-done | bytes 4194320 | tf_op jit(solution)/shard_map/all_gather | solution.py:84
  423.7 70.0 %all-gather.26.cloned.1.call-done = bf16[1024,2048]{1,0:T(8,128)(2,1)} async-done(((bf16[256,2048]{1,0:T(8,128)(2,1)}), bf16[1024,2048]{1,0:T(8,128)(2,1)}) %all-gather.26.cloned.1.call-update) | async-done | bytes 4194320 | tf_op jit(solution)/shard_map/all_gather | solution.py:84
  498.9 75.3 %all-gather.18.cloned.1.call-done = bf16[1024,2048]{0,1:T(8,128)(2,1)} async-done(((bf16[256,2048]{0,1:T(8,128)(2,1)}), bf16[1024,2048]{0,1:T(8,128)(2,1)}) %all-gather.18.cloned.1.call-update) | async-done | bytes 4194320 | tf_op jit(solution)/shard_map/all_gather | solution.py:83
  586.8 68.1 %all-gather.28.cloned.1.call-done = bf16[1024,2048]{0,1:T(8,128)(2,1)} async-done(((bf16[256,2048]{0,1:T(8,128)(2,1)}), bf16[1024,2048]{0,1:T(8,128)(2,1)}) %all-gather.28.cloned.1.call-update) | async-done | bytes 4194320 | tf_op jit(solution)/shard_map/all_gather | solution.py:83
  688.7 14.8 multiply_reduce_fusion.7
  703.5 11.0 fusion.15
  724.0 18.3 multiply_reduce_fusion.6
  742.4 26.8 multiply_convert_fusion.7
  769.2 6.0 multiply_convert_fusion.17
  782.5 6.2 fusion.231
  798.1 14.0 multiply_reduce_fusion.3
  812.1 11.0 fusion.19
  832.5 18.6 multiply_reduce_fusion.2
  851.1 27.0 multiply_convert_fusion.3
  878.1 6.0 multiply_convert_fusion.13
  891.3 5.9 fusion.100
  897.2 5.9 fusion.103
  911.2 5.9 fusion.115
  917.1 5.9 fusion.118
  948.2 8.6 fusion.142
  969.3 10.6 add_convert_fusion.3
  1014.6 31.2 reduce-scatter.15.cloned.1.call-done
  1045.9 20.5 fusion.190
  1066.4 59.6 %reduce-scatter.19.cloned.1.call-done = bf16[256,2048]{0,1:T(8,128)(2,1)} async-done(((bf16[1024,2048]{0,1:T(8,128)(2,1)}), bf16[256,2048]{0,1:T(8,128)(2,1)}) %reduce-scatter.19.cloned.1.call-update) | async-done | bytes 1048592 | tf_op jit(solution)/shard_map/reduce_scatter | solution.py:189
  1126.0 32.0 %add_convert_fusion.2 = bf16[2048,6144]{1,0:T(8,128)(2,1)} fusion(f32[2048,6144]{1,0:T(8,128)} %fusion.190, bf16[256,2048]{0,1:T(8,128)(2,1)} %reduce-scatter.19.cloned.1.call-done, bf16[256,2048]{0,1:T(8,128)(2,1)} %bitcast.429, bf16[256,2048]{0,1:T(8,128)(2,1)S(1)} %bitcast.426, f32[256]{0:T(256)S(1)} %copy-done.110, f32[256]{0:T(256)S(1)} %copy-done.107, ...), kind=kOutput, calls=%fused_computation.2 | convolution fusion | flops 6480199680 | bytes 79710208 | tf_op jit(solution)/shard_map/dot_general | solution.py:13
  1158.7 8.5 all_gather.61
  1167.1 258.5 %all-gather.22.cloned.1.call-done = bf16[2048,8192]{1,0:T(8,128)(2,1)} async-done(((bf16[512,8192]{1,0:T(8,128)(2,1)}), bf16[2048,8192]{1,0:T(8,128)(2,1)}) %all-gather.22.cloned.1.call-update) | async-done | bytes 33554448 | tf_op jit(solution)/shard_map/all_gather | solution.py:253
  1425.7 21.7 convolution_add_fusion.1
  1447.3 19.0 convolution_add_fusion
  1466.3 258.3 %all-gather.24.cloned.1.call-done = bf16[8192,2048]{1,0:T(8,128)(2,1)} async-done(((bf16[2048,2048]{1,0:T(8,128)(2,1)}), bf16[8192,2048]{1,0:T(8,128)(2,1)}) %all-gather.24.cloned.1.call-update) | async-done | bytes 33554448 | tf_op jit(solution)/shard_map/all_gather | solution.py:255
  1724.6 21.7 convert_reduce_fusion.1
  1746.4 22.1 convert_reduce_fusion
  1768.5 27.0 fusion.207
  1795.5 37.4 %add_convert_fusion.1 = bf16[2048,8192]{1,0:T(8,128)(2,1)} fusion(f32[2048,8192]{1,0:T(8,128)} %fusion.207, bf16[256,8192]{1,0:T(8,128)(2,1)} %get-tuple-element.162, f32[256]{0:T(256)S(1)} %copy-done.110, f32[256]{0:T(256)S(1)} %copy-done.107, f32[2048]{0:T(1024)S(1)} %bitcast.481, f32[2048]{0:T(1024)S(1)} %bitcast.469, ...), kind=kOutput, calls=%fused_computation.1 | convolution fusion | flops 8626634752 | bytes 105924608 | tf_op jit(solution)/shard_map/dot_general | solution.py:13
  1833.0 30.1 fusion.192
  1863.0 39.8 %add_convert_fusion = bf16[8192,2048]{1,0:T(8,128)(2,1)} fusion(f32[8192,2048]{1,0:T(8,128)} %fusion.192, f32[256]{0:T(256)S(1)} %copy-done.154, bf16[1,2,256,2048]{3,2,1,0:T(8,128)(2,1)} %param.15, f32[256,8192]{1,0:T(8,128)} %convolution_add_fusion), kind=kOutput, calls=%fused_computation | convolution fusion | flops 8643936256 | bytes 110101504 | tf_op jit(solution)/shard_map/dot_general | solution.py:13
  1906.1 8.0 all-gather.3
  1914.1 7.6 all-gather.4
  1921.8 7.1 fusion.56
  1929.0 7.4 fusion.54
  1936.4 20.3 fusion.77
  1956.7 20.9 fusion.76
  1980.3 59.7 %reduce-scatter.21.cloned.1.call-done = bf16[512,6144]{1,0:T(8,128)(2,1)} async-done(((bf16[2048,6144]{1,0:T(8,128)(2,1)}), bf16[512,6144]{1,0:T(8,128)(2,1)}) %reduce-scatter.21.cloned.1.call-update) | async-done | bytes 6291472 | tf_op jit(solution)/shard_map/reduce_scatter | solution.py:275
  2040.0 291.6 %reduce-scatter.25.cloned.1.call-done = bf16[512,8192]{1,0:T(8,128)(2,1)} async-done(((bf16[2048,8192]{1,0:T(8,128)(2,1)}), bf16[512,8192]{1,0:T(8,128)(2,1)}) %reduce-scatter.25.cloned.1.call-update) | async-done | bytes 8388624
  2331.6 291.9 %reduce-scatter.27.cloned.1.call-done = bf16[2048,2048]{1,0:T(8,128)(2,1)} async-done(((bf16[8192,2048]{1,0:T(8,128)(2,1)}), bf16[2048,2048]{1,0:T(8,128)(2,1)}) %reduce-scatter.27.cloned.1.call-update) | async-done | bytes 8388624
  2623.5 15.2 fusion.191
  2638.7 13.5 fusion.189
  2652.2 18.1 convolution_add_fusion.4
  2670.4 18.7 fusion.94
  2695.9 15.1 all-reduce.9
  2711.4 29.8 all-reduce.7
  2746.6 373.5 %all-reduce.12.cloned.1.call-done = (bf16[512,6144]{1,0:T(8,128)(2,1)}, bf16[512,2048]{1,0:T(8,128)(2,1)}, bf16[512,8192]{1,0:T(8,128)(2,1)}, bf16[2048,2048]{1,0:T(8,128)(2,1)}) async-done(((bf16[512,6144]{1,0:T(8,128)(2,1)}, bf16[512,2048]{1,0:T(8,128)(2,1)}, bf16[512,8192]{1,0:T(8,128)(2,1)}, bf16[2048,2048]{1,0:T(8,128)(2,1)}), (bf16[512,6144]{1,0:T(8,128)(2,1)}, bf16[512,2048]{1,0:T(8,128)(2,1)}, ...) | async-done | bytes 25165840 | tf_op jit(solution)/shard_map/psum | solution.py:303
  3120.1 11.9 convert_element_type.383
  3132.0 11.8 convert_element_type.389
  3143.8 6.4 convert_element_type.373
  (603 shorter events, 265.2 us)
Async XLA Ops:
  7.2 19.2 copy-start.160
  7.2 26.6 copy-start.2
  7.2 233.2 %all-gather.14.cloned.1.call-start = ((), (), s32[]{:S(2)}) async-start(), calls=%async_computation.8 | async-start | bytes 31457280 | tf_op jit(solution)/shard_map/all_gather | solution.py:249
  8.0 322.0 %all-gather.20.cloned.1.call-start = ((), (), s32[]{:S(2)}) async-start(), calls=%async_computation.11 | async-start | bytes 10485760 | tf_op jit(solution)/shard_map/all_gather | solution.py:251
  8.7 403.6 %all-gather.16.cloned.1.call-start = ((), (), s32[]{:S(2)}) async-start(), calls=%async_computation.9 | async-start | bytes 5242880 | tf_op jit(solution)/shard_map/all_gather | solution.py:84
  18.3 237.9 %copy-start.39 = (f32[4,1,512]{2,1,0:T(1,128)}, f32[4,1,512]{2,1,0:T(1,128)S(1)}, u32[]{:S(2)}) copy-start(f32[4,1,512]{2,1,0:T(1,128)S(1)} %convert_element_type.392) | copy-start | bytes 24580
  26.4 229.8 %copy-start.42 = (f32[4,1,512]{2,1,0:T(1,128)}, f32[4,1,512]{2,1,0:T(1,128)S(1)}, u32[]{:S(2)}) copy-start(f32[4,1,512]{2,1,0:T(1,128)S(1)} %convert_element_type.393) | copy-start | bytes 24580
  34.2 218.1 %copy-start.80 = (f32[256]{0:T(256)}, f32[256]{0:T(256)S(1)}, u32[]{:S(2)}) copy-start(f32[256]{0:T(256)S(1)} %get-tuple-element.164) | copy-start | bytes 3076
  34.2 222.0 %copy-start.106 = (f32[256]{0:T(256)}, f32[256]{0:T(256)S(1)}, u32[]{:S(2)}) copy-start(f32[256]{0:T(256)S(1)} %get-tuple-element.163) | copy-start | bytes 3076
  34.9 217.4 %copy-start.99 = (f32[256]{0:T(256)}, f32[256]{0:T(256)S(1)}, u32[]{:S(2)}) copy-start(f32[256]{0:T(256)S(1)} %add_rsqrt_fusion.1) | copy-start | bytes 3076
  256.1 237.5 %all-gather.26.cloned.1.call-start = ((), (), s32[]{:S(2)}) async-start(), calls=%async_computation.14 | async-start | bytes 5242880 | tf_op jit(solution)/shard_map/all_gather | solution.py:84
  256.2 11.9 copy-start.109
  256.2 15.8 copy-start.164
  271.9 302.2 %all-gather.18.cloned.1.call-start = ((), (), s32[]{:S(2)}) async-start(), calls=%async_computation.10 | async-start | bytes 5242880 | tf_op jit(solution)/shard_map/all_gather | solution.py:83
  272.5 28.4 copy-start.112
  272.5 28.4 copy-start.114
  286.2 368.8 %all-gather.28.cloned.1.call-start = ((), (), s32[]{:S(2)}) async-start(), calls=%async_computation.15 | async-start | bytes 5242880 | tf_op jit(solution)/shard_map/all_gather | solution.py:83
  287.5 42.4 %copy-start.155 = (f32[256]{0:T(256)}, f32[256]{0:T(256)S(1)}, u32[]{:S(2)}) copy-start(f32[256]{0:T(256)S(1)} %compare_convert_fusion.1) | copy-start | bytes 3076
  289.0 49.6 %copy-start.153 = (f32[256]{0:T(256)}, f32[256]{0:T(256)S(1)}, u32[]{:S(2)}) copy-start(f32[256]{0:T(256)S(1)} %compare_convert_fusion) | copy-start | bytes 3076
  293.7 36.3 %copy-start.14 = (bf16[1,2,256,2048]{3,2,1,0:T(8,128)(2,1)S(1)}, bf16[1,2,256,2048]{3,2,1,0:T(8,128)(2,1)}, u32[]{:S(2)}) copy-start(bf16[1,2,256,2048]{3,2,1,0:T(8,128)(2,1)} %param.15) | copy-start | bytes 6291460
  304.6 696.4 %reduce-scatter.13.cloned.1.call-start = ((), (), s32[]{:S(2)}) async-start(), calls=%async_computation.16 | async-start | bytes 5242880 | tf_op jit(solution)/shard_map/reduce_scatter | solution.py:186
  577.9 95.7 %copy-start.27 = (bf16[1024,512]{0,1:T(8,128)(2,1)}, bf16[1024,512]{0,1:T(8,128)(2,1)S(1)}, u32[]{:S(2)}) copy-start(bf16[1024,512]{0,1:T(8,128)(2,1)S(1)} %get-tuple-element.72) | copy-start | bytes 3145732
  577.9 101.5 %copy-start.31 = (bf16[1024,512]{0,1:T(8,128)(2,1)}, bf16[1024,512]{0,1:T(8,128)(2,1)S(1)}, u32[]{:S(2)}) copy-start(bf16[1024,512]{0,1:T(8,128)(2,1)S(1)} %get-tuple-element.74) | copy-start | bytes 3145732
  580.7 78.3 %copy-start.134 = (f32[8,256]{1,0:T(8,128)}, f32[8,256]{1,0:T(8,128)S(1)}, u32[]{:S(2)}) copy-start(f32[8,256]{1,0:T(8,128)S(1)} %get-tuple-element.153) | copy-start | bytes 24580
  782.4 222.5 %reduce-scatter.17.cloned.1.call-start = ((), (), s32[]{:S(2)}) async-start(), calls=%async_computation.18 | async-start | bytes 5242880 | tf_op jit(solution)/shard_map/reduce_scatter | solution.py:186
  812.0 20.4 copy-start.130
  891.2 154.7 %reduce-scatter.15.cloned.1.call-start = ((), (), s32[]{:S(2)}) async-start(), calls=%async_computation.17 | async-start | bytes 5242880 | tf_op jit(solution)/shard_map/reduce_scatter | solution.py:189
  891.3 11.9 slice-start.12
  910.7 215.3 %reduce-scatter.19.cloned.1.call-start = ((), (), s32[]{:S(2)}) async-start(), calls=%async_computation.19 | async-start | bytes 5242880 | tf_op jit(solution)/shard_map/reduce_scatter | solution.py:189
  911.2 11.9 slice-start.16
  930.5 495.1 %all-gather.22.cloned.1.call-start = ((), (), s32[]{:S(2)}) async-start(), calls=%async_computation.12 | async-start | bytes 41943040 | tf_op jit(solution)/shard_map/all_gather | solution.py:253
  931.3 793.4 %all-gather.24.cloned.1.call-start = ((), (), s32[]{:S(2)}) async-start(), calls=%async_computation.13 | async-start | bytes 41943040 | tf_op jit(solution)/shard_map/all_gather | solution.py:255
  931.9 1048.4 %reduce-scatter.23.cloned.1.call-start = ((), (), s32[]{:S(2)}) async-start(), calls=%async_computation.21 | async-start | bytes 10485760 | tf_op jit(solution)/shard_map/reduce_scatter | solution.py:281
  942.3 14.5 slice-start.4
  979.9 1060.1 %reduce-scatter.21.cloned.1.call-start = ((), (), s32[]{:S(2)}) async-start(), calls=%async_computation.20 | async-start | bytes 31457280 | tf_op jit(solution)/shard_map/reduce_scatter | solution.py:275
  1000.1 11.8 copy-start.113
  1000.1 11.8 copy-start.115
  1006.6 39.3 %copy-start.3 = (bf16[1,2,256,2048]{3,2,1,0:T(8,128)(2,1)S(1)}, bf16[1,2,256,2048]{3,2,1,0:T(8,128)(2,1)}, u32[]{:S(2)}) copy-start(bf16[1,2,256,2048]{3,2,1,0:T(8,128)(2,1)} %param.14) | copy-start | bytes 6291460
  1006.6 39.3 %copy-start.40 = (f32[4,1,512]{2,1,0:T(1,128)S(1)}, f32[4,1,512]{2,1,0:T(1,128)}, u32[]{:S(2)}) copy-start(f32[4,1,512]{2,1,0:T(1,128)} %copy-done.39) | copy-start | bytes 24580
  1006.6 39.3 %copy-start.43 = (f32[4,1,512]{2,1,0:T(1,128)S(1)}, f32[4,1,512]{2,1,0:T(1,128)}, u32[]{:S(2)}) copy-start(f32[4,1,512]{2,1,0:T(1,128)} %copy-done.42) | copy-start | bytes 24580
  1006.6 39.3 %copy-start.81 = (f32[256]{0:T(256)S(1)}, f32[256]{0:T(256)}, u32[]{:S(2)}) copy-start(f32[256]{0:T(256)} %copy-done.80) | copy-start | bytes 3076
  1006.6 39.3 %copy-start.100 = (f32[256]{0:T(256)S(1)}, f32[256]{0:T(256)}, u32[]{:S(2)}) copy-start(f32[256]{0:T(256)} %copy-done.99) | copy-start | bytes 3076
  1013.4 112.6 %copy-start.17 = (bf16[256,32,64]{0,2,1:T(8,128)(2,1)}, bf16[256,32,64]{0,2,1:T(8,128)(2,1)S(1)}, u32[]{:S(2)}) copy-start(bf16[256,32,64]{0,2,1:T(8,128)(2,1)S(1)} %pad_maximum_fusion.16) | copy-start | bytes 3145732
  1045.9 80.1 %copy-start.107 = (f32[256]{0:T(256)S(1)}, f32[256]{0:T(256)}, u32[]{:S(2)}) copy-start(f32[256]{0:T(256)} %copy-done.106) | copy-start | bytes 3076
  1045.9 80.1 %copy-start.110 = (f32[256]{0:T(256)S(1)}, f32[256]{0:T(256)}, u32[]{:S(2)}) copy-start(f32[256]{0:T(256)} %copy-done.109) | copy-start | bytes 3076
  1158.0 1173.6 %reduce-scatter.25.cloned.1.call-start = ((), (), s32[]{:S(2)}) async-start(), calls=%async_computation.22 | async-start | bytes 41943040
  1447.3 277.3 %copy-start.157 = (f32[256]{0:T(256)S(1)}, f32[256]{0:T(256)}, u32[]{:S(2)}) copy-start(f32[256]{0:T(256)} %copy-done.155) | copy-start | bytes 3076
  1832.9 790.5 %reduce-scatter.27.cloned.1.call-start = ((), (), s32[]{:S(2)}) async-start(), calls=%async_computation.23 | async-start | bytes 41943040
  1902.9 18.9 copy-start.84
  1902.9 18.9 copy-start.86
  1902.9 18.9 copy-start.88
  1902.9 18.9 copy-start.90
  1902.9 1217.2 %all-reduce.12.cloned.1.call-start = ((), (), s32[]{:S(2)}) async-start(), calls=%async_computation.24 | async-start | bytes 50331648 | tf_op jit(solution)/shard_map/psum | solution.py:303
  2623.5 15.2 copy-start.18
  2652.2 18.1 copy-start.41
  2652.2 18.1 copy-start.82
  2652.2 18.1 copy-start.101
  2652.2 18.1 copy-start.108
  2652.2 18.1 copy-start.111
  2670.4 18.8 copy-start.16
  2670.4 18.8 copy-start.64
  2742.4 410.4 %copy-start.158 = (f32[512]{0:T(512)}, f32[512]{0:T(512)S(1)}, u32[]{:S(2)}) copy-start(f32[512]{0:T(512)S(1)} %convert_element_type.381) | copy-start | bytes 6148
  3120.1 23.7 slice-start.24
  3132.0 11.8 slice-start.25
  (147 other events, 923.9 us)
Sparse Core Ops, SparseCore 0:
  9.9 230.4 all-gather.13
  242.3 87.6 all-gather.19
  331.5 80.7 all-gather.15
  414.3 79.2 all-gather.25
  495.0 79.0 all-gather.17
  576.2 78.7 all-gather.27
  782.5 74.9 reduce-scatter.12
  891.3 74.8 reduce-scatter.16
  968.6 77.2 reduce-scatter.14
  1048.7 77.2 reduce-scatter.18
  1127.8 297.7 all-gather.21
  1427.4 297.2 all-gather.23
  1728.2 86.4 reduce-scatter.22
  1818.0 221.9 reduce-scatter.20
  2042.9 288.6 reduce-scatter.24
  2334.8 288.6 reduce-scatter.26
  2626.2 493.8 all-reduce.11
where the time goes:
time: 3170 us; the launch traced here: 3160 us
  waiting for transfers between devices  2120 us (67%)
  matrix products  665 us (21%)
  other arithmetic  161 us (5%)
  local copies, waits for them, and re-layouts  95.3 us (3%)
  blocking collectives  93.9 us (3%)
    unnamed x19, waiting for transfers between devices  586 us
    psum x1, waiting for transfers between devices, body(): lax.psum(summed[2].astype(jnp.bfloat16), ('dp', 'ctx')).astype(jnp.float32)  374 us
    all_gather x1, waiting for transfers between devices, body(): lax.all_gather(w_up, 'fsdp', axis=0, tiled=True)  259 us
    all_gather x1, waiting for transfers between devices, body(): lax.all_gather(w_down, 'fsdp', axis=0, tiled=True)  258 us
    dot_general x8, matrix products, contract_rows(): lax.dot_general(left, right, (((0,), (0,)), ((), ())), preferred_element_...  206 us
    all_gather x1, waiting for transfers between devices, body(): lax.all_gather(w_qkv, 'fsdp', axis=0, tiled=True)  206 us
    all_gather x2, waiting for transfers between devices, layer_step(): lax.all_gather(keyed, 'ctx', axis=0, tiled=True)  143 us
    all_gather x2, waiting for transfers between devices, layer_step(): lax.all_gather(valued, 'ctx', axis=0, tiled=True)  124 us
  transfers between devices with their start and end apart: 17, of which 14 were waited for; matrix products, arithmetic and copies ran while one was open for 24% of the time, Pallas kernels for 0%

commit v1 on v0

--- a/solution.py
+++ b/solution.py
@@ -300,7 +300,7 @@
     totals = (
         lax.psum(summed[0].astype(jnp.bfloat16), ("dp", "ctx")).astype(jnp.float32),
         lax.psum(summed[1].astype(jnp.bfloat16), ("dp", "ctx")).astype(jnp.float32),
-        lax.psum(summed[2].astype(jnp.bfloat16), ("dp", "ctx")).astype(jnp.float32),
+        lax.psum(lax.psum(summed[2].astype(jnp.bfloat16), "ctx"), "dp").astype(jnp.float32),
         lax.psum(summed[3].astype(jnp.bfloat16), ("dp", "ctx")).astype(jnp.float32),
         lax.psum(summed[4].astype(jnp.bfloat16), ("dp", "ctx")).astype(jnp.float32),
         lax.psum(summed[5].astype(jnp.bfloat16), ("dp", "ctx")).astype(jnp.float32),

time: 3170 us -> 3330 us (1.050)
  waiting for transfers between devices: 2120 us -> 2280 us
    reduce_scatter x1, waiting for transfers between devices: 59.7 us -> 187 us  [body(): lax.psum_scatter(summed[2].astype(jnp.bfloat16), 'fsdp', scatter_dimensio...]
    psum x1 -> x3, waiting for transfers between devices: 374 us -> 313 us  [the longest x1 293 us: body(): lax.psum(summed[4].astype(jnp.bfloat16), ('dp', 'ctx')).astype(jnp.float32)]
    reduce_scatter x2, waiting for transfers between devices: 90.9 us -> 129 us  [layer_step(): lax.psum_scatter(values_grad_all.astype(jnp.bfloat16), 'ctx', scatter_dim...]
    unnamed x19 -> x21, waiting for transfers between devices: 586 us -> 586 us
  transfers between devices with their start and end apart: 17 -> 19, of which waited for: 14 -> 17; matrix products, arithmetic and copies ran while one was open for 24% -> 22% of each run, Pallas kernels for 0% -> 0%
where the time goes in v1:
time: 3330 us; the launch traced here: 3320 us
  waiting for transfers between devices  2280 us (68%)
  matrix products  660 us (20%)
  other arithmetic  166 us (5%)
  local copies, waits for them, and re-layouts  100 us (3%)
  blocking collectives  93.5 us (3%)
    unnamed x21, waiting for transfers between devices  586 us
    psum x1, waiting for transfers between devices, body(): lax.psum(summed[4].astype(jnp.bfloat16), ('dp', 'ctx')).astype(jnp.float32)  293 us
    all_gather x1, waiting for transfers between devices, body(): lax.all_gather(w_up, 'fsdp', axis=0, tiled=True)  264 us
    all_gather x1, waiting for transfers between devices, body(): lax.all_gather(w_down, 'fsdp', axis=0, tiled=True)  259 us
    all_gather x1, waiting for transfers between devices, body(): lax.all_gather(w_qkv, 'fsdp', axis=0, tiled=True)  206 us
    dot_general x8, matrix products, contract_rows(): lax.dot_general(left, right, (((0,), (0,)), ((), ())), preferred_element_...  195 us
    reduce_scatter x1, waiting for transfers between devices, body(): lax.psum_scatter(summed[2].astype(jnp.bfloat16), 'fsdp', scatter_dimensio...  187 us
    all_gather x2, waiting for transfers between devices, layer_step(): lax.all_gather(keyed, 'ctx', axis=0, tiled=True)  143 us
  transfers between devices with their start and end apart: 19, of which 17 were waited for; matrix products, arithmetic and copies ran while one was open for 22% of the time, Pallas kernels for 0%

profile of v1, /device:TPU:0, one launch (start us, length us, event | category | flops | bytes accessed | tf_op | source)
XLA Modules:
  0.0 3318.2 jit_solution(12919504704390750034)
XLA Ops:
  8.8 9.6 all-gather.2
  18.4 8.0 all-gather.1
  26.5 7.1 all-gather
  34.8 205.6 %all-gather.14.cloned.1.call-done = bf16[2048,6144]{1,0:T(8,128)(2,1)} async-done(((bf16[512,6144]{1,0:T(8,128)(2,1)}), bf16[2048,6144]{1,0:T(8,128)(2,1)}) %all-gather.14.cloned.1.call-update) | async-done | bytes 25165840 | tf_op jit(solution)/shard_map/all_gather | solution.py:249
  240.4 11.8 convolution_add_fusion.2
  256.2 11.8 convolution_add_fusion.3
  306.0 23.9 all-gather.20.cloned.1.call-done
  338.5 6.4 convolution_convert_fusion.1
  358.4 54.4 %all-gather.26.cloned.1.call-done = bf16[1024,2048]{1,0:T(8,128)(2,1)} async-done(((bf16[256,2048]{1,0:T(8,128)(2,1)}), bf16[1024,2048]{1,0:T(8,128)(2,1)}) %all-gather.26.cloned.1.call-update) | async-done | bytes 4194320 | tf_op jit(solution)/shard_map/all_gather | solution.py:84
  424.1 69.5 %all-gather.16.cloned.1.call-done = bf16[1024,2048]{1,0:T(8,128)(2,1)} async-done(((bf16[256,2048]{1,0:T(8,128)(2,1)}), bf16[1024,2048]{1,0:T(8,128)(2,1)}) %all-gather.16.cloned.1.call-update) | async-done | bytes 4194320 | tf_op jit(solution)/shard_map/all_gather | solution.py:84
  498.8 75.3 %all-gather.28.cloned.1.call-done = bf16[1024,2048]{0,1:T(8,128)(2,1)} async-done(((bf16[256,2048]{0,1:T(8,128)(2,1)}), bf16[1024,2048]{0,1:T(8,128)(2,1)}) %all-gather.28.cloned.1.call-update) | async-done | bytes 4194320 | tf_op jit(solution)/shard_map/all_gather | solution.py:83
  586.7 68.2 %all-gather.18.cloned.1.call-done = bf16[1024,2048]{0,1:T(8,128)(2,1)} async-done(((bf16[256,2048]{0,1:T(8,128)(2,1)}), bf16[1024,2048]{0,1:T(8,128)(2,1)}) %all-gather.18.cloned.1.call-update) | async-done | bytes 4194320 | tf_op jit(solution)/shard_map/all_gather | solution.py:83
  688.3 14.3 multiply_reduce_fusion.3
  702.6 11.0 fusion.19
  723.0 18.4 multiply_reduce_fusion.2
  741.4 26.8 multiply_convert_fusion.3
  768.2 6.0 multiply_convert_fusion.10
  781.5 6.2 fusion.229
  797.0 14.0 multiply_reduce_fusion.7
  811.0 11.0 fusion.15
  831.4 18.6 multiply_reduce_fusion.6
  850.0 27.0 multiply_convert_fusion.7
  877.0 5.9 multiply_convert_fusion.14
  890.2 5.9 fusion.109
  954.9 10.3 reduce-scatter.13.cloned.1.call-done
  975.7 69.0 %reduce-scatter.15.cloned.1.call-done = bf16[256,2048]{0,1:T(8,128)(2,1)} async-done(((bf16[1024,2048]{0,1:T(8,128)(2,1)}), bf16[256,2048]{0,1:T(8,128)(2,1)}) %reduce-scatter.15.cloned.1.call-update) | async-done | bytes 1048592 | tf_op jit(solution)/shard_map/reduce_scatter | solution.py:189
  1044.8 20.5 fusion.190
  1065.3 59.6 %reduce-scatter.19.cloned.1.call-done = bf16[256,2048]{0,1:T(8,128)(2,1)} async-done(((bf16[1024,2048]{0,1:T(8,128)(2,1)}), bf16[256,2048]{0,1:T(8,128)(2,1)}) %reduce-scatter.19.cloned.1.call-update) | async-done | bytes 1048592 | tf_op jit(solution)/shard_map/reduce_scatter | solution.py:189
  1124.9 25.8 add_convert_fusion.2
  1152.2 8.1 all_gather.61
  1177.6 8.6 fusion.142
  1186.2 187.0 %reduce-scatter.21.cloned.1.call-done = bf16[512,6144]{1,0:T(8,128)(2,1)} async-done(((bf16[2048,6144]{1,0:T(8,128)(2,1)}), bf16[512,6144]{1,0:T(8,128)(2,1)}) %reduce-scatter.21.cloned.1.call-update) | async-done | bytes 6291472 | tf_op jit(solution)/shard_map/reduce_scatter | solution.py:275
  1379.1 6.2 fusion.133
  1395.5 12.1 add_convert_fusion.3
  1407.9 264.5 %all-gather.22.cloned.1.call-done = bf16[2048,8192]{1,0:T(8,128)(2,1)} async-done(((bf16[512,8192]{1,0:T(8,128)(2,1)}), bf16[2048,8192]{1,0:T(8,128)(2,1)}) %all-gather.22.cloned.1.call-update) | async-done | bytes 33554448 | tf_op jit(solution)/shard_map/all_gather | solution.py:253
  1672.4 21.2 convolution_add_fusion
  1693.5 19.3 convolution_add_fusion.1
  1712.9 258.7 %all-gather.24.cloned.1.call-done = bf16[8192,2048]{1,0:T(8,128)(2,1)} async-done(((bf16[2048,2048]{1,0:T(8,128)(2,1)}), bf16[8192,2048]{1,0:T(8,128)(2,1)}) %all-gather.24.cloned.1.call-update) | async-done | bytes 33554448 | tf_op jit(solution)/shard_map/all_gather | solution.py:255
  1971.6 21.8 convert_reduce_fusion
  1993.4 21.9 convert_reduce_fusion.1
  2015.4 25.8 fusion.207
  2041.1 34.5 %add_convert_fusion.1 = bf16[2048,8192]{1,0:T(8,128)(2,1)} fusion(f32[2048,8192]{1,0:T(8,128)} %fusion.207, bf16[256,8192]{1,0:T(8,128)(2,1)} %get-tuple-element.161, f32[256]{0:T(256)S(1)} %copy-done.111, f32[256]{0:T(256)S(1)} %copy-done.108, f32[2048]{0:T(1024)S(1)} %bitcast.475, f32[2048]{0:T(1024)S(1)} %bitcast.465, ...), kind=kOutput, calls=%fused_computation.1 | convolution fusion | flops 8626634752 | bytes 105924608 | tf_op jit(solution)/shard_map/dot_general | solution.py:13
  2075.7 29.9 fusion.192
  2105.6 37.7 %add_convert_fusion = bf16[8192,2048]{1,0:T(8,128)(2,1)} fusion(f32[8192,2048]{1,0:T(8,128)} %fusion.192, f32[256]{0:T(256)S(1)} %copy-done.156, bf16[1,2,256,2048]{3,2,1,0:T(8,128)(2,1)} %param.15, f32[256,8192]{1,0:T(8,128)} %convolution_add_fusion), kind=kOutput, calls=%fused_computation | convolution fusion | flops 8643936256 | bytes 110101504 | tf_op jit(solution)/shard_map/dot_general | solution.py:13
  2144.0 8.1 all-gather.3
  2152.1 7.3 all-gather.4
  2162.1 7.2 fusion.54
  2169.3 7.1 fusion.56
  2176.4 20.4 all-reduce.14.cloned.1.call-done
  2196.9 20.4 fusion.76
  2217.4 21.0 fusion.77
  2241.4 13.9 fusion.189
  2255.2 30.7 reduce-scatter.23.cloned.1.call-done
  2286.0 291.6 %reduce-scatter.25.cloned.1.call-done = bf16[512,8192]{1,0:T(8,128)(2,1)} async-done(((bf16[2048,8192]{1,0:T(8,128)(2,1)}), bf16[512,8192]{1,0:T(8,128)(2,1)}) %reduce-scatter.25.cloned.1.call-update) | async-done | bytes 8388624
  2577.6 291.9 %reduce-scatter.27.cloned.1.call-done = bf16[2048,2048]{1,0:T(8,128)(2,1)} async-done(((bf16[8192,2048]{1,0:T(8,128)(2,1)}), bf16[2048,2048]{1,0:T(8,128)(2,1)}) %reduce-scatter.27.cloned.1.call-update) | async-done | bytes 8388624
  2869.5 14.3 fusion.191
  2883.8 19.8 convolution_add_fusion.4
  2903.7 19.2 fusion.94
  2929.8 15.3 all-reduce.9
  2945.4 29.8 all-reduce.7
  2980.7 9.3 convert_element_type.373
  2990.0 293.1 %all-reduce.18.cloned.1.call-done = (bf16[512,2048]{1,0:T(8,128)(2,1)}, bf16[512,8192]{1,0:T(8,128)(2,1)}, bf16[2048,2048]{1,0:T(8,128)(2,1)}) async-done(((bf16[512,2048]{1,0:T(8,128)(2,1)}, bf16[512,8192]{1,0:T(8,128)(2,1)}, bf16[2048,2048]{1,0:T(8,128)(2,1)}), (bf16[512,2048]{1,0:T(8,128)(2,1)}, bf16[512,8192]{1,0:T(8,128)(2,1)}, bf16[2048,2048]{1,0:T(8,128)(2,1)})) %all-reduce.18.cloned.1.call-update) | async-done | bytes 18874384 | tf_op jit(solution)/shard_map/psum | solution.py:305
  3287.2 11.7 convert_element_type.383
  3298.9 11.7 convert_element_type.389
  (596 shorter events, 295.7 us)
Async XLA Ops:
  7.2 19.3 copy-start.164
  7.2 26.4 copy-start.2
  7.2 233.2 %all-gather.14.cloned.1.call-start = ((), (), s32[]{:S(2)}) async-start(), calls=%async_computation.8 | async-start | bytes 31457280 | tf_op jit(solution)/shard_map/all_gather | solution.py:249
  8.0 321.9 %all-gather.20.cloned.1.call-start = ((), (), s32[]{:S(2)}) async-start(), calls=%async_computation.11 | async-start | bytes 10485760 | tf_op jit(solution)/shard_map/all_gather | solution.py:251
  8.7 404.1 %all-gather.26.cloned.1.call-start = ((), (), s32[]{:S(2)}) async-start(), calls=%async_computation.14 | async-start | bytes 5242880 | tf_op jit(solution)/shard_map/all_gather | solution.py:84
  26.5 229.6 %copy-start.42 = (f32[4,1,512]{2,1,0:T(1,128)}, f32[4,1,512]{2,1,0:T(1,128)S(1)}, u32[]{:S(2)}) copy-start(f32[4,1,512]{2,1,0:T(1,128)S(1)} %convert_element_type.393) | copy-start | bytes 24580
  33.7 222.5 %copy-start.39 = (f32[4,1,512]{2,1,0:T(1,128)}, f32[4,1,512]{2,1,0:T(1,128)S(1)}, u32[]{:S(2)}) copy-start(f32[4,1,512]{2,1,0:T(1,128)S(1)} %convert_element_type.392) | copy-start | bytes 24580
  34.0 218.2 %copy-start.107 = (f32[256]{0:T(256)}, f32[256]{0:T(256)S(1)}, u32[]{:S(2)}) copy-start(f32[256]{0:T(256)S(1)} %get-tuple-element.162) | copy-start | bytes 3076
  34.0 222.1 %copy-start.79 = (f32[256]{0:T(256)}, f32[256]{0:T(256)S(1)}, u32[]{:S(2)}) copy-start(f32[256]{0:T(256)S(1)} %get-tuple-element.163) | copy-start | bytes 3076
  34.7 217.5 %copy-start.110 = (f32[256]{0:T(256)}, f32[256]{0:T(256)S(1)}, u32[]{:S(2)}) copy-start(f32[256]{0:T(256)S(1)} %add_rsqrt_fusion) | copy-start | bytes 3076
  256.1 237.5 %all-gather.16.cloned.1.call-start = ((), (), s32[]{:S(2)}) async-start(), calls=%async_computation.9 | async-start | bytes 5242880 | tf_op jit(solution)/shard_map/all_gather | solution.py:84
  271.9 302.2 %all-gather.28.cloned.1.call-start = ((), (), s32[]{:S(2)}) async-start(), calls=%async_computation.15 | async-start | bytes 5242880 | tf_op jit(solution)/shard_map/all_gather | solution.py:83
  272.4 28.3 copy-start.113
  272.4 28.3 copy-start.115
  286.0 368.9 %all-gather.18.cloned.1.call-start = ((), (), s32[]{:S(2)}) async-start(), calls=%async_computation.10 | async-start | bytes 5242880 | tf_op jit(solution)/shard_map/all_gather | solution.py:83
  287.4 42.5 %copy-start.155 = (f32[256]{0:T(256)}, f32[256]{0:T(256)S(1)}, u32[]{:S(2)}) copy-start(f32[256]{0:T(256)S(1)} %compare_convert_fusion) | copy-start | bytes 3076
  288.8 49.7 %copy-start.157 = (f32[256]{0:T(256)}, f32[256]{0:T(256)S(1)}, u32[]{:S(2)}) copy-start(f32[256]{0:T(256)S(1)} %compare_convert_fusion.1) | copy-start | bytes 3076
  293.5 36.4 %copy-start.14 = (bf16[1,2,256,2048]{3,2,1,0:T(8,128)(2,1)S(1)}, bf16[1,2,256,2048]{3,2,1,0:T(8,128)(2,1)}, u32[]{:S(2)}) copy-start(bf16[1,2,256,2048]{3,2,1,0:T(8,128)(2,1)} %param.15) | copy-start | bytes 6291460
  304.5 645.8 %reduce-scatter.17.cloned.1.call-start = ((), (), s32[]{:S(2)}) async-start(), calls=%async_computation.18 | async-start | bytes 5242880 | tf_op jit(solution)/shard_map/reduce_scatter | solution.py:186
  358.4 300.4 %copy-start.56 = (bf16[256,512]{0,1:T(8,128)(2,1)}, bf16[256,512]{0,1:T(8,128)(2,1)S(1)}, u32[]{:S(2)}) copy-start(bf16[256,512]{0,1:T(8,128)(2,1)S(1)} %get-tuple-element.112) | copy-start | bytes 786436
  577.7 95.5 %copy-start.31 = (bf16[1024,512]{0,1:T(8,128)(2,1)}, bf16[1024,512]{0,1:T(8,128)(2,1)S(1)}, u32[]{:S(2)}) copy-start(bf16[1024,512]{0,1:T(8,128)(2,1)S(1)} %get-tuple-element.80) | copy-start | bytes 3145732
  577.8 101.3 %copy-start.24 = (bf16[1024,512]{0,1:T(8,128)(2,1)}, bf16[1024,512]{0,1:T(8,128)(2,1)S(1)}, u32[]{:S(2)}) copy-start(bf16[1024,512]{0,1:T(8,128)(2,1)S(1)} %get-tuple-element.81) | copy-start | bytes 3145732
  781.4 183.8 %reduce-scatter.13.cloned.1.call-start = ((), (), s32[]{:S(2)}) async-start(), calls=%async_computation.16 | async-start | bytes 5242880 | tf_op jit(solution)/shard_map/reduce_scatter | solution.py:186
  811.0 20.4 copy-start.127
  890.2 154.6 %reduce-scatter.15.cloned.1.call-start = ((), (), s32[]{:S(2)}) async-start(), calls=%async_computation.17 | async-start | bytes 5242880 | tf_op jit(solution)/shard_map/reduce_scatter | solution.py:189
  909.6 215.3 %reduce-scatter.19.cloned.1.call-start = ((), (), s32[]{:S(2)}) async-start(), calls=%async_computation.19 | async-start | bytes 5242880 | tf_op jit(solution)/shard_map/reduce_scatter | solution.py:189
  929.4 443.9 %reduce-scatter.21.cloned.1.call-start = ((), (), s32[]{:S(2)}) async-start(), calls=%async_computation.20 | async-start | bytes 31457280 | tf_op jit(solution)/shard_map/reduce_scatter | solution.py:275
  946.4 21.7 copy-start.118
  946.4 21.7 copy-start.120
  949.4 23.8 copy-start.114
  949.4 23.8 copy-start.116
  966.4 78.3 %copy-start.3 = (bf16[1,2,256,2048]{3,2,1,0:T(8,128)(2,1)S(1)}, bf16[1,2,256,2048]{3,2,1,0:T(8,128)(2,1)}, u32[]{:S(2)}) copy-start(bf16[1,2,256,2048]{3,2,1,0:T(8,128)(2,1)} %param.14) | copy-start | bytes 6291460
  966.4 78.3 %copy-start.40 = (f32[4,1,512]{2,1,0:T(1,128)S(1)}, f32[4,1,512]{2,1,0:T(1,128)}, u32[]{:S(2)}) copy-start(f32[4,1,512]{2,1,0:T(1,128)} %copy-done.39) | copy-start | bytes 24580
  966.4 78.3 %copy-start.43 = (f32[4,1,512]{2,1,0:T(1,128)S(1)}, f32[4,1,512]{2,1,0:T(1,128)}, u32[]{:S(2)}) copy-start(f32[4,1,512]{2,1,0:T(1,128)} %copy-done.42) | copy-start | bytes 24580
  966.5 78.3 %copy-start.80 = (f32[256]{0:T(256)S(1)}, f32[256]{0:T(256)}, u32[]{:S(2)}) copy-start(f32[256]{0:T(256)} %copy-done.79) | copy-start | bytes 3076
  966.5 78.3 %copy-start.100 = (f32[256]{0:T(256)S(1)}, f32[256]{0:T(256)}, u32[]{:S(2)}) copy-start(f32[256]{0:T(256)} %copy-done.99) | copy-start | bytes 3076
  1044.8 80.1 %copy-start.108 = (f32[256]{0:T(256)S(1)}, f32[256]{0:T(256)}, u32[]{:S(2)}) copy-start(f32[256]{0:T(256)} %copy-done.107) | copy-start | bytes 3076
  1044.8 80.1 %copy-start.111 = (f32[256]{0:T(256)S(1)}, f32[256]{0:T(256)}, u32[]{:S(2)}) copy-start(f32[256]{0:T(256)} %copy-done.110) | copy-start | bytes 3076
  1150.8 521.6 %all-gather.22.cloned.1.call-start = ((), (), s32[]{:S(2)}) async-start(), calls=%async_computation.12 | async-start | bytes 41943040 | tf_op jit(solution)/shard_map/all_gather | solution.py:253
  1151.4 820.2 %all-gather.24.cloned.1.call-start = ((), (), s32[]{:S(2)}) async-start(), calls=%async_computation.13 | async-start | bytes 41943040 | tf_op jit(solution)/shard_map/all_gather | solution.py:255
  1152.1 1044.7 %all-reduce.14.cloned.1.call-start = ((), (), s32[]{:S(2)}) async-start(), calls=%async_computation.21 | async-start | bytes 12582912 | tf_op jit(solution)/shard_map/psum | solution.py:303
  1177.6 196.1 %copy-start.126 = (f32[8,256]{1,0:T(8,128)S(1)}, f32[8,256]{1,0:T(8,128)}, u32[]{:S(2)}) copy-start(f32[8,256]{1,0:T(8,128)} %copy-done.125) | copy-start | bytes 24580
  1177.6 196.1 %copy-start.142 = (f32[8,256]{1,0:T(8,128)S(1)}, f32[8,256]{1,0:T(8,128)}, u32[]{:S(2)}) copy-start(f32[8,256]{1,0:T(8,128)} %copy-done.141) | copy-start | bytes 24580
  1373.3 912.7 %reduce-scatter.23.cloned.1.call-start = ((), (), s32[]{:S(2)}) async-start(), calls=%async_computation.23 | async-start | bytes 10485760 | tf_op jit(solution)/shard_map/reduce_scatter | solution.py:281
  1407.6 285.9 %copy-start.81 = (f32[256]{0:T(256)S(1)}, f32[256]{0:T(256)}, u32[]{:S(2)}) copy-start(f32[256]{0:T(256)} %copy-done.79) | copy-start | bytes 3076
  1407.6 285.9 %copy-start.101 = (f32[256]{0:T(256)S(1)}, f32[256]{0:T(256)}, u32[]{:S(2)}) copy-start(f32[256]{0:T(256)} %copy-done.99) | copy-start | bytes 3076
  1407.6 1169.9 %reduce-scatter.25.cloned.1.call-start = ((), (), s32[]{:S(2)}) async-start(), calls=%async_computation.24 | async-start | bytes 41943040
  2075.7 793.8 %reduce-scatter.27.cloned.1.call-start = ((), (), s32[]{:S(2)}) async-start(), calls=%async_computation.25 | async-start | bytes 41943040
  2143.3 18.7 copy-start.92
  2143.3 18.7 copy-start.94
  2143.3 18.7 copy-start.96
  2143.4 837.3 %all-reduce.16.cloned.1.call-start = ((), (), s32[]{:S(2)}) async-start(), calls=%async_computation.22 | async-start | bytes 12582912 | tf_op jit(solution)/shard_map/psum | solution.py:303
  2196.8 1086.2 %all-reduce.18.cloned.1.call-start = ((), (), s32[]{:S(2)}) async-start(), calls=%async_computation.26 | async-start | bytes 37748736 | tf_op jit(solution)/shard_map/psum | solution.py:305
  2196.9 20.4 copy-start.149
  2196.9 20.4 copy-start.150
  2217.3 24.0 copy-start.18
  2883.8 19.8 copy-start.41
  2883.8 19.8 copy-start.82
  2883.8 19.8 copy-start.102
  2883.8 19.8 copy-start.109
  2883.8 19.8 copy-start.112
  2903.6 19.4 copy-start.17
  2903.7 19.4 copy-start.63
  2977.0 333.6 %copy-start.159 = (f32[512]{0:T(512)}, f32[512]{0:T(512)S(1)}, u32[]{:S(2)}) copy-start(f32[512]{0:T(512)S(1)} %convert_element_type.381) | copy-start | bytes 6148
  (144 other events, 1008.0 us)
Sparse Core Ops, SparseCore 0:
  9.9 230.4 all-gather.13
  242.2 87.5 all-gather.19
  332.0 80.7 all-gather.25
  414.3 79.2 all-gather.15
  495.0 79.0 all-gather.27
  576.1 78.7 all-gather.17
  781.6 74.9 reduce-scatter.16
  890.3 74.8 reduce-scatter.12
  967.5 77.2 reduce-scatter.14
  1047.6 77.2 reduce-scatter.18
  1150.9 222.3 reduce-scatter.20
  1375.1 297.2 all-gather.21
  1674.3 297.2 all-gather.23
  1973.9 222.8 all-reduce.13
  2200.6 85.3 reduce-scatter.22
  2288.9 288.6 reduce-scatter.24
  2580.8 288.6 reduce-scatter.26
  2871.8 31.9 all-reduce.15
  2906.9 376.0 all-reduce.17
